TPU v7x, 32 devices: a whole 2x2x4 slice. The times are simulated.
32 devices in a mesh: ctx: 8 (over z, x), tp: 4 (over y, core).
Axes of the slice: x: 2, y: 2, z: 4, core: 2. Of those that a mesh axis runs over, the one named last changes fastest.
Arguments:
- q_raw: bfloat16 [2048, 4096], P('ctx', 'tp'), may hold values from -36 to 36
- k_raw: bfloat16 [2048, 2048], P('ctx', 'tp'), may hold values from -36 to 36
- v_cur: bfloat16 [2048, 2048], P('ctx', 'tp'), may hold values from -6 to 6
- d_out: bfloat16 [2048, 4096], P('ctx', 'tp'), may hold values from -6 to 6
- q_gain: float32 [128], replicated, may hold values from 0.25 to 1.75
- k_gain: float32 [128], replicated, may hold values from 0.25 to 1.75
Outputs:
- dq_raw: bfloat16 [2048, 4096], P('ctx', 'tp')
- dk_raw: bfloat16 [2048, 2048], P('ctx', 'tp')
- dv: bfloat16 [2048, 2048], P('ctx', 'tp')
- q_gain_grad: float32 [128], replicated
- k_gain_grad: float32 [128], replicated
All inputs are finite; a program needn't handle non-finite values.
Results may differ from a plain program's by a relative error of at most 0.0077.
Values may be sent and summed in bfloat16 or wider, within the bound.
A program may use at most 64 MiB of HBM per device.

v0:
```python
import jax
import jax.numpy as jnp
from jax import lax
from jax.sharding import PartitionSpec as P

Q_HEADS = 32
KV_HEADS = 16
HEAD_DIM = 128
WINDOW = 1024
score_scale = 168.0 ** (-0.5)
epsilon = 1e-06


def shifted(value, axis, by):
    devices = lax.axis_size(axis)
    pairs = [(i, i + by) for i in range(devices) if 0 <= i + by < devices]
    return lax.ppermute(value, axis, pairs)


def normalize(raw32, gain):
    vectors = raw32.reshape(raw32.shape[0], -1, HEAD_DIM)
    inverse = lax.rsqrt(jnp.mean(vectors * vectors, axis=-1, keepdims=True) + epsilon)
    return vectors * inverse * gain


def per_device(q_raw, k_raw, v_cur, d_out, q_gain, k_gain):
    row_count = q_raw.shape[0]
    hop_count = WINDOW // row_count
    q_normed, pull_query = jax.vjp(normalize, q_raw.astype(jnp.float32), q_gain)
    k_normed, pull_key = jax.vjp(normalize, k_raw.astype(jnp.float32), k_gain)
    q_low = q_normed.astype(jnp.bfloat16)
    k_low = k_normed.astype(jnp.bfloat16)
    local_kv = k_low.shape[1]
    local_q = q_low.shape[1]
    group = local_q // local_kv
    value_low = v_cur.reshape(row_count, local_kv, HEAD_DIM)
    grad_out = d_out.reshape(row_count, local_q, HEAD_DIM)
    earlier = []
    for distance in range(1, hop_count + 1):
        earlier.append(shifted((k_low, value_low), "ctx", distance))
    band_keys = jnp.concatenate(
        [earlier[d][0] for d in reversed(range(hop_count))] + [k_low], axis=0
    )
    band_values = jnp.concatenate(
        [earlier[d][1] for d in reversed(range(hop_count))] + [value_low], axis=0
    )
    band_width = (hop_count + 1) * row_count
    device_index = lax.axis_index("ctx")
    row_ids = lax.broadcasted_iota(jnp.int32, (row_count, band_width), 0)
    col_ids = lax.broadcasted_iota(jnp.int32, (row_count, band_width), 1)
    distance_ids = row_ids + hop_count * row_count - col_ids
    band_start = (device_index - hop_count) * row_count
    visible = (distance_ids >= 0) & (distance_ids < WINDOW) & (band_start + col_ids >= 0)
    dq_parts = []
    dk_parts = []
    dv_parts = []
    for kv_head in range(local_kv):
        queries = q_low[:, kv_head * group : (kv_head + 1) * group]
        grads = grad_out[:, kv_head * group : (kv_head + 1) * group]
        head_keys = band_keys[:, kv_head]
        head_values = band_values[:, kv_head]
        scores = (
            jnp.einsum("tgd,cd->gtc", queries, head_keys, preferred_element_type=jnp.float32)
            * score_scale
        )
        exp_scores = jnp.where(visible, jnp.exp(scores), 0.0)
        probs = exp_scores / jnp.sum(exp_scores, axis=-1, keepdims=True)
        dprobs = jnp.einsum("tgd,cd->gtc", grads, head_values, preferred_element_type=jnp.float32)
        row_delta = jnp.sum(probs * dprobs, axis=-1, keepdims=True)
        dscores = (probs * (dprobs - row_delta) * score_scale).astype(jnp.bfloat16)
        probs_low = probs.astype(jnp.bfloat16)
        dq_parts.append(
            jnp.einsum("gtc,cd->tgd", dscores, head_keys, preferred_element_type=jnp.float32)
        )
        dk_parts.append(
            jnp.einsum("gtc,tgd->cd", dscores, queries, preferred_element_type=jnp.float32).astype(
                jnp.bfloat16
            )
        )
        dv_parts.append(
            jnp.einsum("gtc,tgd->cd", probs_low, grads, preferred_element_type=jnp.float32).astype(
                jnp.bfloat16
            )
        )
    query_grad = jnp.concatenate(dq_parts, axis=1)
    key_blocks = jnp.stack(dk_parts, axis=1).reshape(hop_count + 1, row_count, local_kv, HEAD_DIM)
    value_blocks = jnp.stack(dv_parts, axis=1).reshape(hop_count + 1, row_count, local_kv, HEAD_DIM)
    key_grad = key_blocks[hop_count].astype(jnp.float32)
    value_grad = value_blocks[hop_count].astype(jnp.float32)
    for distance in range(1, hop_count + 1):
        got_key, got_value = shifted(
            (key_blocks[hop_count - distance], value_blocks[hop_count - distance]), "ctx", -distance
        )
        key_grad = key_grad + got_key.astype(jnp.float32)
        value_grad = value_grad + got_value.astype(jnp.float32)
    dq_raw32, q_gain_part = pull_query(query_grad)
    dk_raw32, k_gain_part = pull_key(key_grad)
    gain_totals = lax.psum((q_gain_part, k_gain_part), ("ctx", "tp"))
    token_total = row_count * lax.axis_size("ctx")
    q_gain_grad = gain_totals[0] / jnp.sqrt(jnp.float32(token_total * Q_HEADS))
    k_gain_grad = gain_totals[1] / jnp.sqrt(jnp.float32(token_total * KV_HEADS))
    dq_raw = dq_raw32.astype(jnp.bfloat16)
    dk_raw = dk_raw32.astype(jnp.bfloat16)
    dv = value_grad.reshape(row_count, -1).astype(jnp.bfloat16)
    return (dq_raw, dk_raw, dv, q_gain_grad, k_gain_grad)


def solution(mesh):
    return jax.shard_map(
        per_device,
        mesh=mesh,
        in_specs=(P("ctx", "tp"), P("ctx", "tp"), P("ctx", "tp"), P("ctx", "tp"), P(), P()),
        out_specs=(P("ctx", "tp"), P("ctx", "tp"), P("ctx", "tp"), P(), P()),
        check_vma=False,
    )
```

profile of v0, /device:TPU:0, one launch (start us, length us, event | category | flops | bytes accessed | tf_op | source)
XLA Modules:
  0.0 263.9 jit_solution(4225913662095262754)
XLA Ops:
  2.0 5.5 %collective-permute-start.7 = (bf16[256,4,128]{2,0,1:T(8,128)(2,1)S(1)}, bf16[256,4,128]{2,0,1:T(8,128)(2,1)}, u32[]{:S(2)}, u32[]{:S(2)}) collective-permute-start(bf16[256,4,128]{2,0,1:T(8,128)(2,1)S(1)} %copy.106), channel_id=1, source_target_pairs={{0,4},{4,8},{8,12},{12,16},{16,20},{20,24},{24,28},{1,5},{5,9},{9,... | collective-permute-start | bytes 786440 | tf_op jit(solution)/shard_map/ppermute | solution.py:17
  7.5 3.5 %collective-permute-start.6 = (bf16[256,4,128]{2,0,1:T(8,128)(2,1)S(1)}, bf16[256,4,128]{2,0,1:T(8,128)(2,1)}, u32[]{:S(2)}, u32[]{:S(2)}) collective-permute-start(bf16[256,4,128]{2,0,1:T(8,128)(2,1)S(1)} %copy.106), channel_id=1, source_target_pairs={{0,8},{4,12},{8,16},{12,20},{16,24},{20,28},{1,9},{5,13},{9,17},{1... | collective-permute-start | bytes 786440 | tf_op jit(solution)/shard_map/ppermute | solution.py:17
  13.3 3.6 %collective-permute-start.2 = (bf16[256,4,128]{2,0,1:T(8,128)(2,1)}, bf16[256,4,128]{2,0,1:T(8,128)(2,1)}, u32[]{:S(2)}, u32[]{:S(2)}) collective-permute-start(bf16[256,4,128]{2,0,1:T(8,128)(2,1)} %multiply_convert_fusion.1), channel_id=1, source_target_pairs={{0,8},{4,12},{8,16},{12,20},{16,24},{20,28},{1,9},{5,13},{9,17},{1... | collective-permute-start | bytes 786440 | tf_op jit(solution)/shard_map/ppermute | solution.py:17
  16.9 2.9 %collective-permute-start.1 = (bf16[256,4,128]{2,0,1:T(8,128)(2,1)}, bf16[256,4,128]{2,0,1:T(8,128)(2,1)}, u32[]{:S(2)}, u32[]{:S(2)}) collective-permute-start(bf16[256,4,128]{2,0,1:T(8,128)(2,1)} %multiply_convert_fusion.1), channel_id=1, source_target_pairs={{0,12},{4,16},{8,20},{12,24},{16,28},{1,13},{5,17},{9,21},{13,25},... | collective-permute-start | bytes 786440 | tf_op jit(solution)/shard_map/ppermute | solution.py:17
  19.8 2.0 collective-permute-start
  24.8 8.0 %collective-permute-done = bf16[256,4,128]{2,0,1:T(8,128)(2,1)} collective-permute-done((bf16[256,4,128]{2,0,1:T(8,128)(2,1)}, bf16[256,4,128]{2,0,1:T(8,128)(2,1)}, u32[]{:S(2)}, u32[]{:S(2)}) %collective-permute-start) | collective-permute-done | bytes 262176 | tf_op jit(solution)/shard_map/ppermute | solution.py:17
  32.8 5.7 %collective-permute-start.3 = (bf16[256,4,128]{2,0,1:T(8,128)(2,1)}, bf16[256,4,128]{2,0,1:T(8,128)(2,1)S(1)}, u32[]{:S(2)}, u32[]{:S(2)}) collective-permute-start(bf16[256,4,128]{2,0,1:T(8,128)(2,1)} %multiply_convert_fusion.1), channel_id=1, source_target_pairs={{0,4},{4,8},{8,12},{12,16},{16,20},{20,24},{24,28},{1,5},{5,9},{9,... | collective-permute-start | bytes 786440 | tf_op jit(solution)/shard_map/ppermute | solution.py:17
  38.5 1.7 constant_dynamic-update-slice_fusion.4
  40.2 16.8 %collective-permute-start.5 = (bf16[256,4,128]{2,0,1:T(8,128)(2,1)S(1)}, bf16[256,4,128]{2,0,1:T(8,128)(2,1)}, u32[]{:S(2)}, u32[]{:S(2)}) collective-permute-start(bf16[256,4,128]{2,0,1:T(8,128)(2,1)S(1)} %copy.106), channel_id=1, source_target_pairs={{0,12},{4,16},{8,20},{12,24},{16,28},{1,13},{5,17},{9,21},{13,25},... | collective-permute-start | bytes 786440 | tf_op jit(solution)/shard_map/ppermute | solution.py:17
  56.9 1.7 constant_dynamic-update-slice_fusion.3
  58.6 14.0 %collective-permute-start.4 = (bf16[256,4,128]{2,0,1:T(8,128)(2,1)S(1)}, bf16[256,4,128]{2,0,1:T(8,128)(2,1)}, u32[]{:S(2)}, u32[]{:S(2)}) collective-permute-start(bf16[256,4,128]{2,0,1:T(8,128)(2,1)S(1)} %copy.106), channel_id=1, source_target_pairs={{0,16},{4,20},{8,24},{12,28},{1,17},{5,21},{9,25},{13,29},{2,18},{... | collective-permute-start | bytes 786440 | tf_op jit(solution)/shard_map/ppermute | solution.py:17
  72.7 1.7 constant_dynamic-update-slice_fusion.2
  76.1 3.5 %fusion.77 = f32[2,256,1280]{1,2,0:T(8,128)} fusion(pred[256,1280]{0,1:T(8,128)(4,1)} %fusion.95, bf16[1280,4,128]{2,0,1:T(8,128)(2,1)} %constant_dynamic-update-slice_fusion, bf16[256,8,128]{2,0,1:T(8,128)(2,1)S(1)} %copy-done.7), kind=kOutput, calls=%fused_computation.86 | convolution fusion | flops 169740032 | bytes 3407872 | tf_op jit(solution)/shard_map/div | solution.py:67
  79.6 3.5 %fusion.79 = f32[2,256,1280]{1,2,0:T(8,128)} fusion(pred[256,1280]{0,1:T(8,128)(4,1)} %fusion.95, bf16[1280,4,128]{2,0,1:T(8,128)(2,1)} %constant_dynamic-update-slice_fusion, bf16[256,8,128]{2,0,1:T(8,128)(2,1)S(1)} %copy-done.7), kind=kOutput, calls=%fused_computation.88 | convolution fusion | flops 169740032 | bytes 3407872 | tf_op jit(solution)/shard_map/div | solution.py:67
  83.0 3.5 %fusion.81 = f32[2,256,1280]{1,2,0:T(8,128)} fusion(pred[256,1280]{0,1:T(8,128)(4,1)} %fusion.95, bf16[1280,4,128]{2,0,1:T(8,128)(2,1)} %constant_dynamic-update-slice_fusion, bf16[256,8,128]{2,0,1:T(8,128)(2,1)S(1)} %copy-done.7), kind=kOutput, calls=%fused_computation.90 | convolution fusion | flops 169740032 | bytes 3407872 | tf_op jit(solution)/shard_map/div | solution.py:67
  86.5 3.5 %fusion.91 = f32[2,256,1280]{1,2,0:T(8,128)} fusion(pred[256,1280]{0,1:T(8,128)(4,1)} %fusion.95, bf16[1280,4,128]{2,0,1:T(8,128)(2,1)} %constant_dynamic-update-slice_fusion, bf16[256,8,128]{2,0,1:T(8,128)(2,1)S(1)} %copy-done.7), kind=kOutput, calls=%fused_computation.100 | convolution fusion | flops 169740032 | bytes 3407872 | tf_op jit(solution)/shard_map/div | solution.py:67
  94.2 1.3 fusion.44
  95.5 2.0 convolution_bitcast_fusion
  97.5 5.8 %fusion.96 = f32[256,2,128]{2,0,1:T(8,128)} fusion(f32[2,256,1280]{1,2,0:T(8,128)} %fusion.77, f32[2,256,1280]{1,2,0:T(8,128)} %convolution_bitcast_fusion, bf16[1280,4,128]{2,0,1:T(8,128)(2,1)} %constant_dynamic-update-slice_fusion), kind=kOutput, calls=%fused_computation.106 | convolution fusion | flops 171050752 | bytes 11075584 | tf_op jit(solution)/shard_map/gtc,cd->tgd/dot_general | solution.py:73
  103.3 5.6 %fusion.48 = bf16[1280,1,128]{2,0,1:T(8,128)(2,1)} fusion(f32[2,256,1280]{1,2,0:T(8,128)} %fusion.77, f32[2,256,1280]{1,2,0:T(8,128)} %convolution_bitcast_fusion, bf16[256,8,128]{2,0,1:T(8,128)(2,1)S(1)} %copy-done.7), kind=kOutput, calls=%fused_computation.68 | convolution fusion | flops 171214592 | bytes 10944512 | tf_op jit(solution)/shard_map/gtc,tgd->cd/dot_general | solution.py:76
  108.9 3.2 %convolution_bitcast_fusion.1 = f32[2,256,1280]{1,2,0:T(8,128)} fusion(bf16[1280,4,128]{2,0,1:T(8,128)(2,1)} %copy-done.4, bf16[256,8,128]{0,2,1:T(8,128)(2,1)S(1)} %bitcast.191), kind=kOutput, calls=%fused_computation.21 | convolution fusion | flops 167772160 | bytes 3080192 | tf_op jit(solution)/shard_map/tgd,cd->gtc/dot_general | solution.py:68
  112.0 1.3 fusion.45
  113.3 5.8 %fusion.99 = f32[256,2,128]{2,0,1:T(8,128)} fusion(f32[2,256,1280]{1,2,0:T(8,128)} %fusion.79, f32[2,256,1280]{1,2,0:T(8,128)} %convolution_bitcast_fusion.1, bf16[1280,4,128]{2,0,1:T(8,128)(2,1)} %constant_dynamic-update-slice_fusion), kind=kOutput, calls=%fused_computation.107 | convolution fusion | flops 171050752 | bytes 11075584 | tf_op jit(solution)/shard_map/gtc,cd->tgd/dot_general | solution.py:73
  119.1 5.6 %fusion.49 = bf16[1280,1,128]{2,0,1:T(8,128)(2,1)} fusion(f32[2,256,1280]{1,2,0:T(8,128)} %fusion.79, f32[2,256,1280]{1,2,0:T(8,128)} %convolution_bitcast_fusion.1, bf16[256,8,128]{2,0,1:T(8,128)(2,1)S(1)} %copy-done.7), kind=kOutput, calls=%fused_computation.69 | convolution fusion | flops 171214592 | bytes 10944512 | tf_op jit(solution)/shard_map/gtc,tgd->cd/dot_general | solution.py:76
  124.7 3.1 %convolution_bitcast_fusion.2 = f32[2,256,1280]{1,2,0:T(8,128)} fusion(bf16[1280,4,128]{2,0,1:T(8,128)(2,1)} %copy-done.4, bf16[256,8,128]{0,2,1:T(8,128)(2,1)S(1)} %bitcast.193), kind=kOutput, calls=%fused_computation.22 | convolution fusion | flops 167772160 | bytes 3080192 | tf_op jit(solution)/shard_map/tgd,cd->gtc/dot_general | solution.py:68
  127.8 1.3 fusion.46
  129.1 5.8 %fusion.102 = f32[256,2,128]{2,0,1:T(8,128)} fusion(f32[2,256,1280]{1,2,0:T(8,128)} %fusion.81, f32[2,256,1280]{1,2,0:T(8,128)} %convolution_bitcast_fusion.2, bf16[1280,4,128]{2,0,1:T(8,128)(2,1)} %constant_dynamic-update-slice_fusion), kind=kOutput, calls=%fused_computation.108 | convolution fusion | flops 171050752 | bytes 11075584 | tf_op jit(solution)/shard_map/gtc,cd->tgd/dot_general | solution.py:73
  134.9 5.6 %fusion.50 = bf16[1280,1,128]{2,0,1:T(8,128)(2,1)} fusion(f32[2,256,1280]{1,2,0:T(8,128)} %fusion.81, f32[2,256,1280]{1,2,0:T(8,128)} %convolution_bitcast_fusion.2, bf16[256,8,128]{2,0,1:T(8,128)(2,1)S(1)} %copy-done.7), kind=kOutput, calls=%fused_computation.70 | convolution fusion | flops 171214592 | bytes 10944512 | tf_op jit(solution)/shard_map/gtc,tgd->cd/dot_general | solution.py:76
  140.5 3.1 %convolution_bitcast_fusion.3 = f32[2,256,1280]{1,2,0:T(8,128)} fusion(bf16[1280,4,128]{2,0,1:T(8,128)(2,1)} %copy-done.4, bf16[256,8,128]{0,2,1:T(8,128)(2,1)S(1)} %bitcast.195), kind=kOutput, calls=%fused_computation.23 | convolution fusion | flops 167772160 | bytes 3080192 | tf_op jit(solution)/shard_map/tgd,cd->gtc/dot_general | solution.py:68
  144.9 6.0 %fusion.105 = f32[256,2,128]{2,0,1:T(8,128)} fusion(f32[2,256,1280]{1,2,0:T(8,128)} %fusion.91, f32[2,256,1280]{1,2,0:T(8,128)} %convolution_bitcast_fusion.3, bf16[1280,4,128]{2,0,1:T(8,128)(2,1)} %constant_dynamic-update-slice_fusion), kind=kOutput, calls=%fused_computation.109 | convolution fusion | flops 171050752 | bytes 11075584 | tf_op jit(solution)/shard_map/gtc,cd->tgd/dot_general | solution.py:73
  151.0 5.6 %fusion.51 = bf16[1280,1,128]{2,0,1:T(8,128)(2,1)} fusion(f32[2,256,1280]{1,2,0:T(8,128)} %fusion.91, f32[2,256,1280]{1,2,0:T(8,128)} %convolution_bitcast_fusion.3, bf16[256,8,128]{2,0,1:T(8,128)(2,1)S(1)} %copy-done.7), kind=kOutput, calls=%fused_computation.71 | convolution fusion | flops 171214592 | bytes 10944512 | tf_op jit(solution)/shard_map/gtc,tgd->cd/dot_general | solution.py:76
  156.6 1.5 pad_maximum_fusion.1
  159.1 1.3 collective-permute-start.12
  160.4 1.3 collective-permute-start.15
  161.7 1.3 collective-permute-start.14
  163.0 1.3 collective-permute-start.13
  165.6 1.6 copy.128
  168.3 2.0 copy.154
  170.4 1.4 pad_maximum_fusion
  172.8 1.3 collective-permute-start.8
  174.1 1.3 collective-permute-start.11
  175.4 12.9 %collective-permute-done.15 = bf16[256,4,128]{0,2,1:T(8,128)(2,1)} collective-permute-done((bf16[256,4,128]{0,2,1:T(8,128)(2,1)}, bf16[256,4,128]{0,2,1:T(8,128)(2,1)}, u32[]{:S(2)}, u32[]{:S(2)}) %collective-permute-start.15) | collective-permute-done | bytes 262176 | tf_op jit(solution)/shard_map/ppermute | solution.py:17
  188.3 1.3 collective-permute-start.10
  189.6 1.3 collective-permute-start.9
  190.9 1.4 add_convert_fusion
  193.1 23.3 %collective-permute-done.11 = bf16[256,4,128]{2,0,1:T(8,128)(2,1)} collective-permute-done((bf16[256,4,128]{2,0,1:T(8,128)(2,1)}, bf16[256,4,128]{2,0,1:T(8,128)(2,1)}, u32[]{:S(2)}, u32[]{:S(2)}) %collective-permute-start.11) | collective-permute-done | bytes 262176 | tf_op jit(solution)/shard_map/ppermute | solution.py:17
  216.4 1.6 multiply_reduce_fusion.6
  219.3 44.1 %all-reduce = (f32[128]{0:T(128)S(1)}, f32[128]{0:T(128)S(1)}) all-reduce(f32[128]{0:T(128)S(1)} %bitcast_reduce_fusion, f32[128]{0:T(128)S(1)} %get-tuple-element.20), channel_id=1, replica_groups=mesh['ctx'=8,'tp'=4] {'ctx','tp'}, use_global_device_ids=true, to_apply=%region_14.15 | all-reduce | flops 256 | bytes 2048 | tf_op jit(solution)/shard_map/psum | solution.py:98
  (78 shorter events, 20.8 us)
Async XLA Ops:
  0.6 11.7 %copy-start.12 = (f32[128]{0:T(128)S(1)}, f32[128]{0:T(128)}, u32[]{:S(2)}) copy-start(f32[128]{0:T(128)} %param.11) | copy-start | bytes 1540
  0.6 21.1 %copy-start.5 = (bf16[256,1024]{1,0:T(8,128)(2,1)S(1)}, bf16[256,1024]{1,0:T(8,128)(2,1)}, u32[]{:S(2)}) copy-start(bf16[256,1024]{1,0:T(8,128)(2,1)} %param.6) | copy-start | bytes 1572868
  2.0 91.1 %collective-permute-start.7 = (bf16[256,4,128]{2,0,1:T(8,128)(2,1)S(1)}, bf16[256,4,128]{2,0,1:T(8,128)(2,1)}, u32[]{:S(2)}, u32[]{:S(2)}) collective-permute-start(bf16[256,4,128]{2,0,1:T(8,128)(2,1)S(1)} %copy.106), channel_id=1, source_target_pairs={{0,4},{4,8},{8,12},{12,16},{16,20},{20,24},{24,28},{1,5},{5,9},{9,... | collective-permute-start | bytes 786440 | tf_op jit(solution)/shard_map/ppermute | solution.py:17
  7.5 84.6 %collective-permute-start.6 = (bf16[256,4,128]{2,0,1:T(8,128)(2,1)S(1)}, bf16[256,4,128]{2,0,1:T(8,128)(2,1)}, u32[]{:S(2)}, u32[]{:S(2)}) collective-permute-start(bf16[256,4,128]{2,0,1:T(8,128)(2,1)S(1)} %copy.106), channel_id=1, source_target_pairs={{0,8},{4,12},{8,16},{12,20},{16,24},{20,28},{1,9},{5,13},{9,17},{1... | collective-permute-start | bytes 786440 | tf_op jit(solution)/shard_map/ppermute | solution.py:17
  12.1 11.3 %copy-start.13 = (f32[128]{0:T(128)S(1)}, f32[128]{0:T(128)}, u32[]{:S(2)}) copy-start(f32[128]{0:T(128)} %param.10) | copy-start | bytes 1540
  13.3 11.3 %copy-start.6 = (bf16[256,1024]{1,0:T(8,128)(2,1)S(1)}, bf16[256,1024]{1,0:T(8,128)(2,1)}, u32[]{:S(2)}) copy-start(bf16[256,1024]{1,0:T(8,128)(2,1)} %param.9) | copy-start | bytes 1572868
  13.3 45.4 %collective-permute-start.2 = (bf16[256,4,128]{2,0,1:T(8,128)(2,1)}, bf16[256,4,128]{2,0,1:T(8,128)(2,1)}, u32[]{:S(2)}, u32[]{:S(2)}) collective-permute-start(bf16[256,4,128]{2,0,1:T(8,128)(2,1)} %multiply_convert_fusion.1), channel_id=1, source_target_pairs={{0,8},{4,12},{8,16},{12,20},{16,24},{20,28},{1,9},{5,13},{9,17},{1... | collective-permute-start | bytes 786440 | tf_op jit(solution)/shard_map/ppermute | solution.py:17
  16.9 23.3 %collective-permute-start.1 = (bf16[256,4,128]{2,0,1:T(8,128)(2,1)}, bf16[256,4,128]{2,0,1:T(8,128)(2,1)}, u32[]{:S(2)}, u32[]{:S(2)}) collective-permute-start(bf16[256,4,128]{2,0,1:T(8,128)(2,1)} %multiply_convert_fusion.1), channel_id=1, source_target_pairs={{0,12},{4,16},{8,20},{12,24},{16,28},{1,13},{5,17},{9,21},{13,25},... | collective-permute-start | bytes 786440 | tf_op jit(solution)/shard_map/ppermute | solution.py:17
  19.8 13.0 %collective-permute-start = (bf16[256,4,128]{2,0,1:T(8,128)(2,1)}, bf16[256,4,128]{2,0,1:T(8,128)(2,1)}, u32[]{:S(2)}, u32[]{:S(2)}) collective-permute-start(bf16[256,4,128]{2,0,1:T(8,128)(2,1)} %multiply_convert_fusion.1), channel_id=1, source_target_pairs={{0,16},{4,20},{8,24},{12,28},{1,17},{5,21},{9,25},{13,29},{2,18},{... | collective-permute-start | bytes 786440 | tf_op jit(solution)/shard_map/ppermute | solution.py:17
  24.8 51.2 %copy-start.7 = (bf16[256,8,128]{2,0,1:T(8,128)(2,1)S(1)}, bf16[256,8,128]{2,0,1:T(8,128)(2,1)}, u32[]{:S(2)}) copy-start(bf16[256,8,128]{2,0,1:T(8,128)(2,1)} %multiply_convert_fusion) | copy-start | bytes 1572868
  32.8 41.6 %collective-permute-start.3 = (bf16[256,4,128]{2,0,1:T(8,128)(2,1)}, bf16[256,4,128]{2,0,1:T(8,128)(2,1)S(1)}, u32[]{:S(2)}, u32[]{:S(2)}) collective-permute-start(bf16[256,4,128]{2,0,1:T(8,128)(2,1)} %multiply_convert_fusion.1), channel_id=1, source_target_pairs={{0,4},{4,8},{8,12},{12,16},{16,20},{20,24},{24,28},{1,5},{5,9},{9,... | collective-permute-start | bytes 786440 | tf_op jit(solution)/shard_map/ppermute | solution.py:17
  40.2 51.0 %collective-permute-start.5 = (bf16[256,4,128]{2,0,1:T(8,128)(2,1)S(1)}, bf16[256,4,128]{2,0,1:T(8,128)(2,1)}, u32[]{:S(2)}, u32[]{:S(2)}) collective-permute-start(bf16[256,4,128]{2,0,1:T(8,128)(2,1)S(1)} %copy.106), channel_id=1, source_target_pairs={{0,12},{4,16},{8,20},{12,24},{16,28},{1,13},{5,17},{9,21},{13,25},... | collective-permute-start | bytes 786440 | tf_op jit(solution)/shard_map/ppermute | solution.py:17
  58.6 31.4 %collective-permute-start.4 = (bf16[256,4,128]{2,0,1:T(8,128)(2,1)S(1)}, bf16[256,4,128]{2,0,1:T(8,128)(2,1)}, u32[]{:S(2)}, u32[]{:S(2)}) collective-permute-start(bf16[256,4,128]{2,0,1:T(8,128)(2,1)S(1)} %copy.106), channel_id=1, source_target_pairs={{0,16},{4,20},{8,24},{12,28},{1,17},{5,21},{9,25},{13,29},{2,18},{... | collective-permute-start | bytes 786440 | tf_op jit(solution)/shard_map/ppermute | solution.py:17
  90.0 4.2 %copy-start.3 = (f32[2,256,1280]{1,2,0:T(8,128)S(1)}, f32[2,256,1280]{1,2,0:T(8,128)}, u32[]{:S(2)}) copy-start(f32[2,256,1280]{1,2,0:T(8,128)} %fusion.77) | copy-start | bytes 7864324
  94.2 1.3 copy-start.4
  108.9 3.2 %copy-start.2 = (f32[2,256,1280]{1,2,0:T(8,128)S(1)}, f32[2,256,1280]{1,2,0:T(8,128)}, u32[]{:S(2)}) copy-start(f32[2,256,1280]{1,2,0:T(8,128)} %fusion.79) | copy-start | bytes 7864324
  124.7 3.1 %copy-start.1 = (f32[2,256,1280]{1,2,0:T(8,128)S(1)}, f32[2,256,1280]{1,2,0:T(8,128)}, u32[]{:S(2)}) copy-start(f32[2,256,1280]{1,2,0:T(8,128)} %fusion.81) | copy-start | bytes 7864324
  140.5 3.1 %copy-start = (f32[2,256,1280]{1,2,0:T(8,128)S(1)}, f32[2,256,1280]{1,2,0:T(8,128)}, u32[]{:S(2)}) copy-start(f32[2,256,1280]{1,2,0:T(8,128)} %fusion.91) | copy-start | bytes 7864324
  156.6 7.7 %copy-start.8 = (f32[256,2,128]{2,0,1:T(8,128)S(1)}, f32[256,2,128]{2,0,1:T(8,128)}, u32[]{:S(2)}) copy-start(f32[256,2,128]{2,0,1:T(8,128)} %fusion.96) | copy-start | bytes 786436
  156.6 7.7 %copy-start.9 = (f32[256,2,128]{2,0,1:T(8,128)S(1)}, f32[256,2,128]{2,0,1:T(8,128)}, u32[]{:S(2)}) copy-start(f32[256,2,128]{2,0,1:T(8,128)} %fusion.99) | copy-start | bytes 786436
  156.6 7.7 %copy-start.10 = (f32[256,2,128]{2,0,1:T(8,128)S(1)}, f32[256,2,128]{2,0,1:T(8,128)}, u32[]{:S(2)}) copy-start(f32[256,2,128]{2,0,1:T(8,128)} %fusion.102) | copy-start | bytes 786436
  156.6 7.7 %copy-start.11 = (f32[256,2,128]{2,0,1:T(8,128)S(1)}, f32[256,2,128]{2,0,1:T(8,128)}, u32[]{:S(2)}) copy-start(f32[256,2,128]{2,0,1:T(8,128)} %fusion.105) | copy-start | bytes 786436
  159.1 15.0 %collective-permute-start.12 = (bf16[256,4,128]{0,2,1:T(8,128)(2,1)}, bf16[256,4,128]{0,2,1:T(8,128)(2,1)}, u32[]{:S(2)}, u32[]{:S(2)}) collective-permute-start(bf16[256,4,128]{0,2,1:T(8,128)(2,1)} %get-tuple-element.27), channel_id=1, source_target_pairs={{4,0},{8,4},{12,8},{16,12},{20,16},{24,20},{28,24},{5,1},{9,5},{13... | collective-permute-start | bytes 786440 | tf_op jit(solution)/shard_map/ppermute | solution.py:17
  160.4 27.9 %collective-permute-start.15 = (bf16[256,4,128]{0,2,1:T(8,128)(2,1)}, bf16[256,4,128]{0,2,1:T(8,128)(2,1)}, u32[]{:S(2)}, u32[]{:S(2)}) collective-permute-start(bf16[256,4,128]{0,2,1:T(8,128)(2,1)} %get-tuple-element.28), channel_id=1, source_target_pairs={{16,0},{20,4},{24,8},{28,12},{17,1},{21,5},{25,9},{29,13},{18,2},{... | collective-permute-start | bytes 786440 | tf_op jit(solution)/shard_map/ppermute | solution.py:17
  161.7 27.9 %collective-permute-start.14 = (bf16[256,4,128]{0,2,1:T(8,128)(2,1)}, bf16[256,4,128]{0,2,1:T(8,128)(2,1)}, u32[]{:S(2)}, u32[]{:S(2)}) collective-permute-start(bf16[256,4,128]{0,2,1:T(8,128)(2,1)} %get-tuple-element.29), channel_id=1, source_target_pairs={{12,0},{16,4},{20,8},{24,12},{28,16},{13,1},{17,5},{21,9},{25,13},... | collective-permute-start | bytes 786440 | tf_op jit(solution)/shard_map/ppermute | solution.py:17
  163.0 27.9 %collective-permute-start.13 = (bf16[256,4,128]{0,2,1:T(8,128)(2,1)}, bf16[256,4,128]{0,2,1:T(8,128)(2,1)}, u32[]{:S(2)}, u32[]{:S(2)}) collective-permute-start(bf16[256,4,128]{0,2,1:T(8,128)(2,1)} %get-tuple-element.30), channel_id=1, source_target_pairs={{8,0},{12,4},{16,8},{20,12},{24,16},{28,20},{9,1},{13,5},{17,9},{2... | collective-permute-start | bytes 786440 | tf_op jit(solution)/shard_map/ppermute | solution.py:17
  172.8 20.3 %collective-permute-start.8 = (bf16[256,4,128]{2,0,1:T(8,128)(2,1)}, bf16[256,4,128]{2,0,1:T(8,128)(2,1)}, u32[]{:S(2)}, u32[]{:S(2)}) collective-permute-start(bf16[256,4,128]{2,0,1:T(8,128)(2,1)} %get-tuple-element.31), channel_id=1, source_target_pairs={{4,0},{8,4},{12,8},{16,12},{20,16},{24,20},{28,24},{5,1},{9,5},{13... | collective-permute-start | bytes 786440 | tf_op jit(solution)/shard_map/ppermute | solution.py:17
  174.1 42.2 %collective-permute-start.11 = (bf16[256,4,128]{2,0,1:T(8,128)(2,1)}, bf16[256,4,128]{2,0,1:T(8,128)(2,1)}, u32[]{:S(2)}, u32[]{:S(2)}) collective-permute-start(bf16[256,4,128]{2,0,1:T(8,128)(2,1)} %get-tuple-element.32), channel_id=1, source_target_pairs={{16,0},{20,4},{24,8},{28,12},{17,1},{21,5},{25,9},{29,13},{18,2},{... | collective-permute-start | bytes 786440 | tf_op jit(solution)/shard_map/ppermute | solution.py:17
  188.3 28.1 %collective-permute-start.10 = (bf16[256,4,128]{2,0,1:T(8,128)(2,1)}, bf16[256,4,128]{2,0,1:T(8,128)(2,1)}, u32[]{:S(2)}, u32[]{:S(2)}) collective-permute-start(bf16[256,4,128]{2,0,1:T(8,128)(2,1)} %get-tuple-element.33), channel_id=1, source_target_pairs={{12,0},{16,4},{20,8},{24,12},{28,16},{13,1},{17,5},{21,9},{25,13},... | collective-permute-start | bytes 786440 | tf_op jit(solution)/shard_map/ppermute | solution.py:17
  189.6 26.8 %collective-permute-start.9 = (bf16[256,4,128]{2,0,1:T(8,128)(2,1)}, bf16[256,4,128]{2,0,1:T(8,128)(2,1)}, u32[]{:S(2)}, u32[]{:S(2)}) collective-permute-start(bf16[256,4,128]{2,0,1:T(8,128)(2,1)} %get-tuple-element.34), channel_id=1, source_target_pairs={{8,0},{12,4},{16,8},{20,12},{24,16},{28,20},{9,1},{13,5},{17,9},{2... | collective-permute-start | bytes 786440 | tf_op jit(solution)/shard_map/ppermute | solution.py:17
where the time goes:
time: 265 us; the launch traced here: 264 us
  matrix products  76.3 us (29%)
  starting transfers between devices  64.3 us (24%)
  waiting for transfers between devices  44.1 us (17%)
  blocking collectives  44.1 us (17%)
  local copies, waits for them, and re-layouts  20.6 us (8%)
  other arithmetic  13.5 us (5%)
    ppermute x16, starting transfers between devices, shifted(): return lax.ppermute(value, axis, pairs)  64.3 us
    ppermute x16, waiting for transfers between devices, shifted(): return lax.ppermute(value, axis, pairs)  44.1 us
    psum x1, blocking collectives, per_device(): gain_totals = lax.psum((q_gain_part, k_gain_part), ('ctx', 'tp'))  44.1 us
    dot_general x4, matrix products, per_device(): jnp.einsum('gtc,cd->tgd', dscores, head_keys, preferred_element_type=jnp....  23.4 us
    dot_general x4, matrix products, per_device(): jnp.einsum('gtc,tgd->cd', dscores, queries, preferred_element_type=jnp.fl...  22.4 us
    unnamed x43, local copies, waits for them, and re-layouts  16.3 us
    div x4, matrix products, per_device(): probs = exp_scores / jnp.sum(exp_scores, axis=-1, keepdims=True)  13.9 us
    dot_general x4, matrix products, per_device(): jnp.einsum('tgd,cd->gtc', grads, head_values, preferred_element_type=jnp....  11.4 us
  transfers between devices with their start and end apart: 16, of which 3 were waited for; matrix products, arithmetic and copies ran while one was open for 15% of the time, Pallas kernels for 0%

commit v1 on v0

--- a/solution.py
+++ b/solution.py
@@ -95,7 +95,7 @@
         value_grad = value_grad + got_value.astype(jnp.float32)
     dq_raw32, q_gain_part = pull_query(query_grad)
     dk_raw32, k_gain_part = pull_key(key_grad)
-    gain_totals = lax.psum((q_gain_part, k_gain_part), ("ctx", "tp"))
+    gain_totals = lax.psum(lax.psum((q_gain_part, k_gain_part), "tp"), "ctx")
     token_total = row_count * lax.axis_size("ctx")
     q_gain_grad = gain_totals[0] / jnp.sqrt(jnp.float32(token_total * Q_HEADS))
     k_gain_grad = gain_totals[1] / jnp.sqrt(jnp.float32(token_total * KV_HEADS))

time: 265 us -> 248 us (0.936)
  blocking collectives: 44.1 us -> 27.2 us
    psum x1 -> x2, blocking collectives: 44.1 us -> 27.2 us  [per_device(): gain_totals = lax.psum(lax.psum((q_gain_part, k_gain_part), 'tp'), 'ctx')]
  transfers between devices with their start and end apart: 16 -> 16, of which waited for: 3 -> 3; matrix products, arithmetic and copies ran while one was open for 15% -> 16% of each run, Pallas kernels for 0% -> 0%
where the time goes in v1:
time: 248 us; the launch traced here: 247 us
  matrix products  76.3 us (31%)
  starting transfers between devices  64.3 us (26%)
  waiting for transfers between devices  44.1 us (18%)
  blocking collectives  27.2 us (11%)
  local copies, waits for them, and re-layouts  20.6 us (8%)
  other arithmetic  13.5 us (5%)
    ppermute x16, starting transfers between devices, shifted(): return lax.ppermute(value, axis, pairs)  64.3 us
    ppermute x16, waiting for transfers between devices, shifted(): return lax.ppermute(value, axis, pairs)  44.1 us
    psum x2, blocking collectives, per_device(): gain_totals = lax.psum(lax.psum((q_gain_part, k_gain_part), 'tp'), 'ctx')  27.2 us
    dot_general x4, matrix products, per_device(): jnp.einsum('gtc,cd->tgd', dscores, head_keys, preferred_element_type=jnp....  23.4 us
    dot_general x4, matrix products, per_device(): jnp.einsum('gtc,tgd->cd', dscores, queries, preferred_element_type=jnp.fl...  22.4 us
    unnamed x43, local copies, waits for them, and re-layouts  16.3 us
    div x4, matrix products, per_device(): probs = exp_scores / jnp.sum(exp_scores, axis=-1, keepdims=True)  13.9 us
    dot_general x4, matrix products, per_device(): jnp.einsum('tgd,cd->gtc', grads, head_values, preferred_element_type=jnp....  11.4 us
  transfers between devices with their start and end apart: 16, of which 3 were waited for; matrix products, arithmetic and copies ran while one was open for 16% of the time, Pallas kernels for 0%

profile of v1, /device:TPU:0, one launch (start us, length us, event | category | flops | bytes accessed | tf_op | source)
XLA Modules:
  0.0 247.1 jit_solution(2533522667933192728)
XLA Ops:
  2.0 5.5 %collective-permute-start.7 = (bf16[256,4,128]{2,0,1:T(8,128)(2,1)S(1)}, bf16[256,4,128]{2,0,1:T(8,128)(2,1)}, u32[]{:S(2)}, u32[]{:S(2)}) collective-permute-start(bf16[256,4,128]{2,0,1:T(8,128)(2,1)S(1)} %copy.106), channel_id=1, source_target_pairs={{0,4},{4,8},{8,12},{12,16},{16,20},{20,24},{24,28},{1,5},{5,9},{9,... | collective-permute-start | bytes 786440 | tf_op jit(solution)/shard_map/ppermute | solution.py:17
  7.5 3.5 %collective-permute-start.6 = (bf16[256,4,128]{2,0,1:T(8,128)(2,1)S(1)}, bf16[256,4,128]{2,0,1:T(8,128)(2,1)}, u32[]{:S(2)}, u32[]{:S(2)}) collective-permute-start(bf16[256,4,128]{2,0,1:T(8,128)(2,1)S(1)} %copy.106), channel_id=1, source_target_pairs={{0,8},{4,12},{8,16},{12,20},{16,24},{20,28},{1,9},{5,13},{9,17},{1... | collective-permute-start | bytes 786440 | tf_op jit(solution)/shard_map/ppermute | solution.py:17
  13.3 3.6 %collective-permute-start.2 = (bf16[256,4,128]{2,0,1:T(8,128)(2,1)}, bf16[256,4,128]{2,0,1:T(8,128)(2,1)}, u32[]{:S(2)}, u32[]{:S(2)}) collective-permute-start(bf16[256,4,128]{2,0,1:T(8,128)(2,1)} %multiply_convert_fusion.1), channel_id=1, source_target_pairs={{0,8},{4,12},{8,16},{12,20},{16,24},{20,28},{1,9},{5,13},{9,17},{1... | collective-permute-start | bytes 786440 | tf_op jit(solution)/shard_map/ppermute | solution.py:17
  16.9 2.9 %collective-permute-start.1 = (bf16[256,4,128]{2,0,1:T(8,128)(2,1)}, bf16[256,4,128]{2,0,1:T(8,128)(2,1)}, u32[]{:S(2)}, u32[]{:S(2)}) collective-permute-start(bf16[256,4,128]{2,0,1:T(8,128)(2,1)} %multiply_convert_fusion.1), channel_id=1, source_target_pairs={{0,12},{4,16},{8,20},{12,24},{16,28},{1,13},{5,17},{9,21},{13,25},... | collective-permute-start | bytes 786440 | tf_op jit(solution)/shard_map/ppermute | solution.py:17
  19.8 2.0 collective-permute-start
  24.8 8.0 %collective-permute-done = bf16[256,4,128]{2,0,1:T(8,128)(2,1)} collective-permute-done((bf16[256,4,128]{2,0,1:T(8,128)(2,1)}, bf16[256,4,128]{2,0,1:T(8,128)(2,1)}, u32[]{:S(2)}, u32[]{:S(2)}) %collective-permute-start) | collective-permute-done | bytes 262176 | tf_op jit(solution)/shard_map/ppermute | solution.py:17
  32.8 5.7 %collective-permute-start.3 = (bf16[256,4,128]{2,0,1:T(8,128)(2,1)}, bf16[256,4,128]{2,0,1:T(8,128)(2,1)S(1)}, u32[]{:S(2)}, u32[]{:S(2)}) collective-permute-start(bf16[256,4,128]{2,0,1:T(8,128)(2,1)} %multiply_convert_fusion.1), channel_id=1, source_target_pairs={{0,4},{4,8},{8,12},{12,16},{16,20},{20,24},{24,28},{1,5},{5,9},{9,... | collective-permute-start | bytes 786440 | tf_op jit(solution)/shard_map/ppermute | solution.py:17
  38.5 1.7 constant_dynamic-update-slice_fusion.4
  40.2 16.8 %collective-permute-start.5 = (bf16[256,4,128]{2,0,1:T(8,128)(2,1)S(1)}, bf16[256,4,128]{2,0,1:T(8,128)(2,1)}, u32[]{:S(2)}, u32[]{:S(2)}) collective-permute-start(bf16[256,4,128]{2,0,1:T(8,128)(2,1)S(1)} %copy.106), channel_id=1, source_target_pairs={{0,12},{4,16},{8,20},{12,24},{16,28},{1,13},{5,17},{9,21},{13,25},... | collective-permute-start | bytes 786440 | tf_op jit(solution)/shard_map/ppermute | solution.py:17
  56.9 1.7 constant_dynamic-update-slice_fusion.3
  58.6 14.0 %collective-permute-start.4 = (bf16[256,4,128]{2,0,1:T(8,128)(2,1)S(1)}, bf16[256,4,128]{2,0,1:T(8,128)(2,1)}, u32[]{:S(2)}, u32[]{:S(2)}) collective-permute-start(bf16[256,4,128]{2,0,1:T(8,128)(2,1)S(1)} %copy.106), channel_id=1, source_target_pairs={{0,16},{4,20},{8,24},{12,28},{1,17},{5,21},{9,25},{13,29},{2,18},{... | collective-permute-start | bytes 786440 | tf_op jit(solution)/shard_map/ppermute | solution.py:17
  72.7 1.7 constant_dynamic-update-slice_fusion.2
  76.1 3.5 %fusion.77 = f32[2,256,1280]{1,2,0:T(8,128)} fusion(pred[256,1280]{0,1:T(8,128)(4,1)} %fusion.95, bf16[1280,4,128]{2,0,1:T(8,128)(2,1)} %constant_dynamic-update-slice_fusion, bf16[256,8,128]{2,0,1:T(8,128)(2,1)S(1)} %copy-done.7), kind=kOutput, calls=%fused_computation.86 | convolution fusion | flops 169740032 | bytes 3407872 | tf_op jit(solution)/shard_map/div | solution.py:67
  79.6 3.5 %fusion.79 = f32[2,256,1280]{1,2,0:T(8,128)} fusion(pred[256,1280]{0,1:T(8,128)(4,1)} %fusion.95, bf16[1280,4,128]{2,0,1:T(8,128)(2,1)} %constant_dynamic-update-slice_fusion, bf16[256,8,128]{2,0,1:T(8,128)(2,1)S(1)} %copy-done.7), kind=kOutput, calls=%fused_computation.88 | convolution fusion | flops 169740032 | bytes 3407872 | tf_op jit(solution)/shard_map/div | solution.py:67
  83.0 3.5 %fusion.81 = f32[2,256,1280]{1,2,0:T(8,128)} fusion(pred[256,1280]{0,1:T(8,128)(4,1)} %fusion.95, bf16[1280,4,128]{2,0,1:T(8,128)(2,1)} %constant_dynamic-update-slice_fusion, bf16[256,8,128]{2,0,1:T(8,128)(2,1)S(1)} %copy-done.7), kind=kOutput, calls=%fused_computation.90 | convolution fusion | flops 169740032 | bytes 3407872 | tf_op jit(solution)/shard_map/div | solution.py:67
  86.5 3.5 %fusion.91 = f32[2,256,1280]{1,2,0:T(8,128)} fusion(pred[256,1280]{0,1:T(8,128)(4,1)} %fusion.95, bf16[1280,4,128]{2,0,1:T(8,128)(2,1)} %constant_dynamic-update-slice_fusion, bf16[256,8,128]{2,0,1:T(8,128)(2,1)S(1)} %copy-done.7), kind=kOutput, calls=%fused_computation.100 | convolution fusion | flops 169740032 | bytes 3407872 | tf_op jit(solution)/shard_map/div | solution.py:67
  94.2 1.3 fusion.44
  95.5 2.0 convolution_bitcast_fusion
  97.5 5.8 %fusion.96 = f32[256,2,128]{2,0,1:T(8,128)} fusion(f32[2,256,1280]{1,2,0:T(8,128)} %fusion.77, f32[2,256,1280]{1,2,0:T(8,128)} %convolution_bitcast_fusion, bf16[1280,4,128]{2,0,1:T(8,128)(2,1)} %constant_dynamic-update-slice_fusion), kind=kOutput, calls=%fused_computation.106 | convolution fusion | flops 171050752 | bytes 11075584 | tf_op jit(solution)/shard_map/gtc,cd->tgd/dot_general | solution.py:73
  103.3 5.6 %fusion.48 = bf16[1280,1,128]{2,0,1:T(8,128)(2,1)} fusion(f32[2,256,1280]{1,2,0:T(8,128)} %fusion.77, f32[2,256,1280]{1,2,0:T(8,128)} %convolution_bitcast_fusion, bf16[256,8,128]{2,0,1:T(8,128)(2,1)S(1)} %copy-done.7), kind=kOutput, calls=%fused_computation.68 | convolution fusion | flops 171214592 | bytes 10944512 | tf_op jit(solution)/shard_map/gtc,tgd->cd/dot_general | solution.py:76
  108.9 3.2 %convolution_bitcast_fusion.1 = f32[2,256,1280]{1,2,0:T(8,128)} fusion(bf16[1280,4,128]{2,0,1:T(8,128)(2,1)} %copy-done.4, bf16[256,8,128]{0,2,1:T(8,128)(2,1)S(1)} %bitcast.191), kind=kOutput, calls=%fused_computation.21 | convolution fusion | flops 167772160 | bytes 3080192 | tf_op jit(solution)/shard_map/tgd,cd->gtc/dot_general | solution.py:68
  112.0 1.3 fusion.45
  113.3 5.8 %fusion.99 = f32[256,2,128]{2,0,1:T(8,128)} fusion(f32[2,256,1280]{1,2,0:T(8,128)} %fusion.79, f32[2,256,1280]{1,2,0:T(8,128)} %convolution_bitcast_fusion.1, bf16[1280,4,128]{2,0,1:T(8,128)(2,1)} %constant_dynamic-update-slice_fusion), kind=kOutput, calls=%fused_computation.107 | convolution fusion | flops 171050752 | bytes 11075584 | tf_op jit(solution)/shard_map/gtc,cd->tgd/dot_general | solution.py:73
  119.1 5.6 %fusion.49 = bf16[1280,1,128]{2,0,1:T(8,128)(2,1)} fusion(f32[2,256,1280]{1,2,0:T(8,128)} %fusion.79, f32[2,256,1280]{1,2,0:T(8,128)} %convolution_bitcast_fusion.1, bf16[256,8,128]{2,0,1:T(8,128)(2,1)S(1)} %copy-done.7), kind=kOutput, calls=%fused_computation.69 | convolution fusion | flops 171214592 | bytes 10944512 | tf_op jit(solution)/shard_map/gtc,tgd->cd/dot_general | solution.py:76
  124.7 3.1 %convolution_bitcast_fusion.2 = f32[2,256,1280]{1,2,0:T(8,128)} fusion(bf16[1280,4,128]{2,0,1:T(8,128)(2,1)} %copy-done.4, bf16[256,8,128]{0,2,1:T(8,128)(2,1)S(1)} %bitcast.193), kind=kOutput, calls=%fused_computation.22 | convolution fusion | flops 167772160 | bytes 3080192 | tf_op jit(solution)/shard_map/tgd,cd->gtc/dot_general | solution.py:68
  127.8 1.3 fusion.46
  129.1 5.8 %fusion.102 = f32[256,2,128]{2,0,1:T(8,128)} fusion(f32[2,256,1280]{1,2,0:T(8,128)} %fusion.81, f32[2,256,1280]{1,2,0:T(8,128)} %convolution_bitcast_fusion.2, bf16[1280,4,128]{2,0,1:T(8,128)(2,1)} %constant_dynamic-update-slice_fusion), kind=kOutput, calls=%fused_computation.108 | convolution fusion | flops 171050752 | bytes 11075584 | tf_op jit(solution)/shard_map/gtc,cd->tgd/dot_general | solution.py:73
  134.9 5.6 %fusion.50 = bf16[1280,1,128]{2,0,1:T(8,128)(2,1)} fusion(f32[2,256,1280]{1,2,0:T(8,128)} %fusion.81, f32[2,256,1280]{1,2,0:T(8,128)} %convolution_bitcast_fusion.2, bf16[256,8,128]{2,0,1:T(8,128)(2,1)S(1)} %copy-done.7), kind=kOutput, calls=%fused_computation.70 | convolution fusion | flops 171214592 | bytes 10944512 | tf_op jit(solution)/shard_map/gtc,tgd->cd/dot_general | solution.py:76
  140.5 3.1 %convolution_bitcast_fusion.3 = f32[2,256,1280]{1,2,0:T(8,128)} fusion(bf16[1280,4,128]{2,0,1:T(8,128)(2,1)} %copy-done.4, bf16[256,8,128]{0,2,1:T(8,128)(2,1)S(1)} %bitcast.195), kind=kOutput, calls=%fused_computation.23 | convolution fusion | flops 167772160 | bytes 3080192 | tf_op jit(solution)/shard_map/tgd,cd->gtc/dot_general | solution.py:68
  144.9 6.0 %fusion.105 = f32[256,2,128]{2,0,1:T(8,128)} fusion(f32[2,256,1280]{1,2,0:T(8,128)} %fusion.91, f32[2,256,1280]{1,2,0:T(8,128)} %convolution_bitcast_fusion.3, bf16[1280,4,128]{2,0,1:T(8,128)(2,1)} %constant_dynamic-update-slice_fusion), kind=kOutput, calls=%fused_computation.109 | convolution fusion | flops 171050752 | bytes 11075584 | tf_op jit(solution)/shard_map/gtc,cd->tgd/dot_general | solution.py:73
  151.0 5.6 %fusion.51 = bf16[1280,1,128]{2,0,1:T(8,128)(2,1)} fusion(f32[2,256,1280]{1,2,0:T(8,128)} %fusion.91, f32[2,256,1280]{1,2,0:T(8,128)} %convolution_bitcast_fusion.3, bf16[256,8,128]{2,0,1:T(8,128)(2,1)S(1)} %copy-done.7), kind=kOutput, calls=%fused_computation.71 | convolution fusion | flops 171214592 | bytes 10944512 | tf_op jit(solution)/shard_map/gtc,tgd->cd/dot_general | solution.py:76
  156.6 1.5 pad_maximum_fusion.1
  159.1 1.3 collective-permute-start.12
  160.4 1.3 collective-permute-start.15
  161.7 1.3 collective-permute-start.14
  163.0 1.3 collective-permute-start.13
  165.6 1.6 copy.128
  168.3 2.0 copy.154
  170.4 1.4 pad_maximum_fusion
  174.1 1.3 collective-permute-start.11
  175.4 12.9 %collective-permute-done.15 = bf16[256,4,128]{0,2,1:T(8,128)(2,1)} collective-permute-done((bf16[256,4,128]{0,2,1:T(8,128)(2,1)}, bf16[256,4,128]{0,2,1:T(8,128)(2,1)}, u32[]{:S(2)}, u32[]{:S(2)}) %collective-permute-start.15) | collective-permute-done | bytes 262176 | tf_op jit(solution)/shard_map/ppermute | solution.py:17
  188.3 1.3 collective-permute-start.10
  189.6 1.3 collective-permute-start.9
  190.9 1.4 add_convert_fusion
  193.1 23.3 %collective-permute-done.11 = bf16[256,4,128]{2,0,1:T(8,128)(2,1)} collective-permute-done((bf16[256,4,128]{2,0,1:T(8,128)(2,1)}, bf16[256,4,128]{2,0,1:T(8,128)(2,1)}, u32[]{:S(2)}, u32[]{:S(2)}) %collective-permute-start.11) | collective-permute-done | bytes 262176 | tf_op jit(solution)/shard_map/ppermute | solution.py:17
  216.4 1.6 multiply_reduce_fusion.6
  219.3 5.6 %all-reduce.1 = (f32[128]{0:T(128)S(1)}, f32[128]{0:T(128)S(1)}) all-reduce(f32[128]{0:T(128)S(1)} %bitcast_reduce_fusion, f32[128]{0:T(128)S(1)} %get-tuple-element.20), channel_id=1, replica_groups=mesh['ctx'=8,'tp'=4] {'tp'}, use_global_device_ids=true, to_apply=%region_14.15 | all-reduce | flops 256 | bytes 2048 | tf_op jit(solution)/shard_map/psum | solution.py:98
  225.0 21.6 %all-reduce = (f32[128]{0:T(128)S(1)}, f32[128]{0:T(128)S(1)}) all-reduce(f32[128]{0:T(128)S(1)} %get-tuple-element.24, f32[128]{0:T(128)S(1)} %get-tuple-element.25), channel_id=1, replica_groups=mesh['ctx'=8,'tp'=4] {'ctx'}, use_global_device_ids=true, to_apply=%region_15.16 | all-reduce | flops 256 | bytes 2048 | tf_op jit(solution)/shard_map/psum | solution.py:98
  (79 shorter events, 22.1 us)
Async XLA Ops:
  0.6 11.7 %copy-start.12 = (f32[128]{0:T(128)S(1)}, f32[128]{0:T(128)}, u32[]{:S(2)}) copy-start(f32[128]{0:T(128)} %param.11) | copy-start | bytes 1540
  0.6 21.1 %copy-start.5 = (bf16[256,1024]{1,0:T(8,128)(2,1)S(1)}, bf16[256,1024]{1,0:T(8,128)(2,1)}, u32[]{:S(2)}) copy-start(bf16[256,1024]{1,0:T(8,128)(2,1)} %param.6) | copy-start | bytes 1572868
  2.0 91.1 %collective-permute-start.7 = (bf16[256,4,128]{2,0,1:T(8,128)(2,1)S(1)}, bf16[256,4,128]{2,0,1:T(8,128)(2,1)}, u32[]{:S(2)}, u32[]{:S(2)}) collective-permute-start(bf16[256,4,128]{2,0,1:T(8,128)(2,1)S(1)} %copy.106), channel_id=1, source_target_pairs={{0,4},{4,8},{8,12},{12,16},{16,20},{20,24},{24,28},{1,5},{5,9},{9,... | collective-permute-start | bytes 786440 | tf_op jit(solution)/shard_map/ppermute | solution.py:17
  7.5 84.6 %collective-permute-start.6 = (bf16[256,4,128]{2,0,1:T(8,128)(2,1)S(1)}, bf16[256,4,128]{2,0,1:T(8,128)(2,1)}, u32[]{:S(2)}, u32[]{:S(2)}) collective-permute-start(bf16[256,4,128]{2,0,1:T(8,128)(2,1)S(1)} %copy.106), channel_id=1, source_target_pairs={{0,8},{4,12},{8,16},{12,20},{16,24},{20,28},{1,9},{5,13},{9,17},{1... | collective-permute-start | bytes 786440 | tf_op jit(solution)/shard_map/ppermute | solution.py:17
  12.1 11.3 %copy-start.13 = (f32[128]{0:T(128)S(1)}, f32[128]{0:T(128)}, u32[]{:S(2)}) copy-start(f32[128]{0:T(128)} %param.10) | copy-start | bytes 1540
  13.3 11.3 %copy-start.6 = (bf16[256,1024]{1,0:T(8,128)(2,1)S(1)}, bf16[256,1024]{1,0:T(8,128)(2,1)}, u32[]{:S(2)}) copy-start(bf16[256,1024]{1,0:T(8,128)(2,1)} %param.9) | copy-start | bytes 1572868
  13.3 45.4 %collective-permute-start.2 = (bf16[256,4,128]{2,0,1:T(8,128)(2,1)}, bf16[256,4,128]{2,0,1:T(8,128)(2,1)}, u32[]{:S(2)}, u32[]{:S(2)}) collective-permute-start(bf16[256,4,128]{2,0,1:T(8,128)(2,1)} %multiply_convert_fusion.1), channel_id=1, source_target_pairs={{0,8},{4,12},{8,16},{12,20},{16,24},{20,28},{1,9},{5,13},{9,17},{1... | collective-permute-start | bytes 786440 | tf_op jit(solution)/shard_map/ppermute | solution.py:17
  16.9 23.3 %collective-permute-start.1 = (bf16[256,4,128]{2,0,1:T(8,128)(2,1)}, bf16[256,4,128]{2,0,1:T(8,128)(2,1)}, u32[]{:S(2)}, u32[]{:S(2)}) collective-permute-start(bf16[256,4,128]{2,0,1:T(8,128)(2,1)} %multiply_convert_fusion.1), channel_id=1, source_target_pairs={{0,12},{4,16},{8,20},{12,24},{16,28},{1,13},{5,17},{9,21},{13,25},... | collective-permute-start | bytes 786440 | tf_op jit(solution)/shard_map/ppermute | solution.py:17
  19.8 13.0 %collective-permute-start = (bf16[256,4,128]{2,0,1:T(8,128)(2,1)}, bf16[256,4,128]{2,0,1:T(8,128)(2,1)}, u32[]{:S(2)}, u32[]{:S(2)}) collective-permute-start(bf16[256,4,128]{2,0,1:T(8,128)(2,1)} %multiply_convert_fusion.1), channel_id=1, source_target_pairs={{0,16},{4,20},{8,24},{12,28},{1,17},{5,21},{9,25},{13,29},{2,18},{... | collective-permute-start | bytes 786440 | tf_op jit(solution)/shard_map/ppermute | solution.py:17
  24.8 51.2 %copy-start.7 = (bf16[256,8,128]{2,0,1:T(8,128)(2,1)S(1)}, bf16[256,8,128]{2,0,1:T(8,128)(2,1)}, u32[]{:S(2)}) copy-start(bf16[256,8,128]{2,0,1:T(8,128)(2,1)} %multiply_convert_fusion) | copy-start | bytes 1572868
  32.8 41.6 %collective-permute-start.3 = (bf16[256,4,128]{2,0,1:T(8,128)(2,1)}, bf16[256,4,128]{2,0,1:T(8,128)(2,1)S(1)}, u32[]{:S(2)}, u32[]{:S(2)}) collective-permute-start(bf16[256,4,128]{2,0,1:T(8,128)(2,1)} %multiply_convert_fusion.1), channel_id=1, source_target_pairs={{0,4},{4,8},{8,12},{12,16},{16,20},{20,24},{24,28},{1,5},{5,9},{9,... | collective-permute-start | bytes 786440 | tf_op jit(solution)/shard_map/ppermute | solution.py:17
  40.2 51.0 %collective-permute-start.5 = (bf16[256,4,128]{2,0,1:T(8,128)(2,1)S(1)}, bf16[256,4,128]{2,0,1:T(8,128)(2,1)}, u32[]{:S(2)}, u32[]{:S(2)}) collective-permute-start(bf16[256,4,128]{2,0,1:T(8,128)(2,1)S(1)} %copy.106), channel_id=1, source_target_pairs={{0,12},{4,16},{8,20},{12,24},{16,28},{1,13},{5,17},{9,21},{13,25},... | collective-permute-start | bytes 786440 | tf_op jit(solution)/shard_map/ppermute | solution.py:17
  58.6 31.4 %collective-permute-start.4 = (bf16[256,4,128]{2,0,1:T(8,128)(2,1)S(1)}, bf16[256,4,128]{2,0,1:T(8,128)(2,1)}, u32[]{:S(2)}, u32[]{:S(2)}) collective-permute-start(bf16[256,4,128]{2,0,1:T(8,128)(2,1)S(1)} %copy.106), channel_id=1, source_target_pairs={{0,16},{4,20},{8,24},{12,28},{1,17},{5,21},{9,25},{13,29},{2,18},{... | collective-permute-start | bytes 786440 | tf_op jit(solution)/shard_map/ppermute | solution.py:17
  90.0 4.2 %copy-start.3 = (f32[2,256,1280]{1,2,0:T(8,128)S(1)}, f32[2,256,1280]{1,2,0:T(8,128)}, u32[]{:S(2)}) copy-start(f32[2,256,1280]{1,2,0:T(8,128)} %fusion.77) | copy-start | bytes 7864324
  94.2 1.3 copy-start.4
  108.9 3.2 %copy-start.2 = (f32[2,256,1280]{1,2,0:T(8,128)S(1)}, f32[2,256,1280]{1,2,0:T(8,128)}, u32[]{:S(2)}) copy-start(f32[2,256,1280]{1,2,0:T(8,128)} %fusion.79) | copy-start | bytes 7864324
  124.7 3.1 %copy-start.1 = (f32[2,256,1280]{1,2,0:T(8,128)S(1)}, f32[2,256,1280]{1,2,0:T(8,128)}, u32[]{:S(2)}) copy-start(f32[2,256,1280]{1,2,0:T(8,128)} %fusion.81) | copy-start | bytes 7864324
  140.5 3.1 %copy-start = (f32[2,256,1280]{1,2,0:T(8,128)S(1)}, f32[2,256,1280]{1,2,0:T(8,128)}, u32[]{:S(2)}) copy-start(f32[2,256,1280]{1,2,0:T(8,128)} %fusion.91) | copy-start | bytes 7864324
  156.6 7.7 %copy-start.8 = (f32[256,2,128]{2,0,1:T(8,128)S(1)}, f32[256,2,128]{2,0,1:T(8,128)}, u32[]{:S(2)}) copy-start(f32[256,2,128]{2,0,1:T(8,128)} %fusion.96) | copy-start | bytes 786436
  156.6 7.7 %copy-start.9 = (f32[256,2,128]{2,0,1:T(8,128)S(1)}, f32[256,2,128]{2,0,1:T(8,128)}, u32[]{:S(2)}) copy-start(f32[256,2,128]{2,0,1:T(8,128)} %fusion.99) | copy-start | bytes 786436
  156.6 7.7 %copy-start.10 = (f32[256,2,128]{2,0,1:T(8,128)S(1)}, f32[256,2,128]{2,0,1:T(8,128)}, u32[]{:S(2)}) copy-start(f32[256,2,128]{2,0,1:T(8,128)} %fusion.102) | copy-start | bytes 786436
  156.6 7.7 %copy-start.11 = (f32[256,2,128]{2,0,1:T(8,128)S(1)}, f32[256,2,128]{2,0,1:T(8,128)}, u32[]{:S(2)}) copy-start(f32[256,2,128]{2,0,1:T(8,128)} %fusion.105) | copy-start | bytes 786436
  159.1 15.0 %collective-permute-start.12 = (bf16[256,4,128]{0,2,1:T(8,128)(2,1)}, bf16[256,4,128]{0,2,1:T(8,128)(2,1)}, u32[]{:S(2)}, u32[]{:S(2)}) collective-permute-start(bf16[256,4,128]{0,2,1:T(8,128)(2,1)} %get-tuple-element.29), channel_id=1, source_target_pairs={{4,0},{8,4},{12,8},{16,12},{20,16},{24,20},{28,24},{5,1},{9,5},{13... | collective-permute-start | bytes 786440 | tf_op jit(solution)/shard_map/ppermute | solution.py:17
  160.4 27.9 %collective-permute-start.15 = (bf16[256,4,128]{0,2,1:T(8,128)(2,1)}, bf16[256,4,128]{0,2,1:T(8,128)(2,1)}, u32[]{:S(2)}, u32[]{:S(2)}) collective-permute-start(bf16[256,4,128]{0,2,1:T(8,128)(2,1)} %get-tuple-element.30), channel_id=1, source_target_pairs={{16,0},{20,4},{24,8},{28,12},{17,1},{21,5},{25,9},{29,13},{18,2},{... | collective-permute-start | bytes 786440 | tf_op jit(solution)/shard_map/ppermute | solution.py:17
  161.7 27.9 %collective-permute-start.14 = (bf16[256,4,128]{0,2,1:T(8,128)(2,1)}, bf16[256,4,128]{0,2,1:T(8,128)(2,1)}, u32[]{:S(2)}, u32[]{:S(2)}) collective-permute-start(bf16[256,4,128]{0,2,1:T(8,128)(2,1)} %get-tuple-element.31), channel_id=1, source_target_pairs={{12,0},{16,4},{20,8},{24,12},{28,16},{13,1},{17,5},{21,9},{25,13},... | collective-permute-start | bytes 786440 | tf_op jit(solution)/shard_map/ppermute | solution.py:17
  163.0 27.9 %collective-permute-start.13 = (bf16[256,4,128]{0,2,1:T(8,128)(2,1)}, bf16[256,4,128]{0,2,1:T(8,128)(2,1)}, u32[]{:S(2)}, u32[]{:S(2)}) collective-permute-start(bf16[256,4,128]{0,2,1:T(8,128)(2,1)} %get-tuple-element.32), channel_id=1, source_target_pairs={{8,0},{12,4},{16,8},{20,12},{24,16},{28,20},{9,1},{13,5},{17,9},{2... | collective-permute-start | bytes 786440 | tf_op jit(solution)/shard_map/ppermute | solution.py:17
  172.8 20.3 %collective-permute-start.8 = (bf16[256,4,128]{2,0,1:T(8,128)(2,1)}, bf16[256,4,128]{2,0,1:T(8,128)(2,1)}, u32[]{:S(2)}, u32[]{:S(2)}) collective-permute-start(bf16[256,4,128]{2,0,1:T(8,128)(2,1)} %get-tuple-element.33), channel_id=1, source_target_pairs={{4,0},{8,4},{12,8},{16,12},{20,16},{24,20},{28,24},{5,1},{9,5},{13... | collective-permute-start | bytes 786440 | tf_op jit(solution)/shard_map/ppermute | solution.py:17
  174.1 42.2 %collective-permute-start.11 = (bf16[256,4,128]{2,0,1:T(8,128)(2,1)}, bf16[256,4,128]{2,0,1:T(8,128)(2,1)}, u32[]{:S(2)}, u32[]{:S(2)}) collective-permute-start(bf16[256,4,128]{2,0,1:T(8,128)(2,1)} %get-tuple-element.34), channel_id=1, source_target_pairs={{16,0},{20,4},{24,8},{28,12},{17,1},{21,5},{25,9},{29,13},{18,2},{... | collective-permute-start | bytes 786440 | tf_op jit(solution)/shard_map/ppermute | solution.py:17
  188.3 28.1 %collective-permute-start.10 = (bf16[256,4,128]{2,0,1:T(8,128)(2,1)}, bf16[256,4,128]{2,0,1:T(8,128)(2,1)}, u32[]{:S(2)}, u32[]{:S(2)}) collective-permute-start(bf16[256,4,128]{2,0,1:T(8,128)(2,1)} %get-tuple-element.35), channel_id=1, source_target_pairs={{12,0},{16,4},{20,8},{24,12},{28,16},{13,1},{17,5},{21,9},{25,13},... | collective-permute-start | bytes 786440 | tf_op jit(solution)/shard_map/ppermute | solution.py:17
  189.6 26.8 %collective-permute-start.9 = (bf16[256,4,128]{2,0,1:T(8,128)(2,1)}, bf16[256,4,128]{2,0,1:T(8,128)(2,1)}, u32[]{:S(2)}, u32[]{:S(2)}) collective-permute-start(bf16[256,4,128]{2,0,1:T(8,128)(2,1)} %get-tuple-element.36), channel_id=1, source_target_pairs={{8,0},{12,4},{16,8},{20,12},{24,16},{28,20},{9,1},{13,5},{17,9},{2... | collective-permute-start | bytes 786440 | tf_op jit(solution)/shard_map/ppermute | solution.py:17
